TPU v7x, 32 devices: a whole 2x2x4 slice. The times are simulated.
32 devices in a mesh: boot: 2 (over x), samp: 16 (over z, y, core).
Axes of the slice: x: 2, y: 2, z: 4, core: 2. Of those that a mesh axis runs over, the one named last changes fastest.
Arguments:
- dosage: bfloat16 [32384, 512], P('samp'), may hold values from 0 to 2, as said below
- residuals: bfloat16 [32384, 1280], P('samp', 'boot'), may hold values from -300 to 300
- maf_bin: int32 [512], replicated, may hold values from 0 to 63
- gene_map: int32 [512], replicated, may hold values from 0 to 31, never falling along the last dimension, each value on 1 to 32 neighbouring positions
- gene_order: int32 [32], replicated, may hold values from 0 to 31, each once
Outputs:
- calibrated: float32 [32, 1280], P('samp', 'boot')
Inputs may be any that keep to these rules, and one draw needn't show every extreme that they name: `dosage`: allele counts 0, 1 or 2. `gene_map`: never falling along the variants; each gene holds 1 to 32 consecutive variants, one gene exactly 32. `gene_order`: each gene once.
All inputs are finite; a program needn't handle non-finite values.
Results may differ from a plain program's by a relative error of at most 0.0003.
Values sent between devices are 32-bit elements; how exact they have to be, the bound alone decides.
A program may use at most 64 MiB of HBM per device.

v0:
```python
import math
import jax
import jax.numpy as jnp
from jax import lax
from jax.sharding import PartitionSpec as P

GENE_DEV = 2
RHOS = 11
MAF_BINS = 64
EPSILON = 1e-05


def variant_weights(maf_bin):
    levels = jnp.arange(MAF_BINS, dtype=jnp.float32)
    weight_table = (1.0 - 0.05 * (levels + 0.5) / MAF_BINS) ** 24
    matches = maf_bin[:, None] == jnp.arange(MAF_BINS, dtype=jnp.int32)[None, :]
    return jnp.sum(
        jnp.where(matches, weight_table[None, :], jnp.zeros_like(weight_table)[None, :]), axis=1
    )


def sample_product(dose_part, residuals):
    return lax.dot_general(
        dose_part, residuals, (((0,), (0,)), ((), ())), preferred_element_type=jnp.float32
    )


def shards(dosage, residuals, maf_bin, gene_map, gene_order):
    sample_total = dosage.shape[0] * lax.axis_size("samp")
    scaling = variant_weights(maf_bin) / math.sqrt(sample_total)
    my_index = lax.axis_index("samp")
    partial_value = sample_product(dosage, residuals) * scaling[:, None]
    scores = lax.psum(partial_value, "samp")
    owned_genes = lax.dynamic_slice_in_dim(gene_order, my_index * GENE_DEV, GENE_DEV)
    member = (owned_genes[:, None] == gene_map[None, :]).astype(jnp.float32)
    stacked = jnp.concatenate([scores, scores * scores], axis=1)
    gene_sums = jnp.dot(
        member, stacked, precision=lax.Precision.HIGHEST, preferred_element_type=jnp.float32
    )
    boot_local = residuals.shape[1]
    burden = gene_sums[:, :boot_local]
    skat = gene_sums[:, boot_local:]
    rho_grid = jnp.arange(RHOS, dtype=jnp.float32) / (RHOS - 1)
    mixtures = (1.0 - rho_grid)[None, :, None] * skat[:, None, :] + rho_grid[None, :, None] * (
        burden * burden
    )[:, None, :]
    boot_total = boot_local * lax.axis_size("boot")
    first_sum, square_sum = lax.psum(
        (jnp.sum(mixtures, axis=2), jnp.sum(mixtures * mixtures, axis=2)), "boot"
    )
    center = first_sum / boot_total
    spread = square_sum / boot_total - center * center
    deviation = mixtures - center[:, :, None]
    zscore = deviation / jnp.sqrt(spread[:, :, None] + EPSILON)
    return jnp.max(zscore, axis=1)


def solution(mesh):
    placed = (P("samp", None), P("samp", "boot"), P(), P(), P())
    return jax.shard_map(
        shards, mesh=mesh, in_specs=placed, out_specs=P("samp", "boot"), check_vma=False
    )
```

profile of v0, /device:TPU:0, one launch (start us, length us, event | category | flops | bytes accessed | tf_op | source)
XLA Modules:
  0.0 128.8 jit_solution(401770869329293279)
XLA Ops:
  6.5 0.0 copy-start
  6.5 0.0 all-reduce.3.cloned.1.call-start
  6.6 0.9 select_reduce_fusion
  7.5 0.8 copy-done
  8.3 0.0 copy-start.3
  8.3 4.5 %convolution_multiply_fusion = f32[512,640]{1,0:T(8,128)} fusion(bf16[2024,512]{1,0:T(8,128)(2,1)} %param.5, bf16[2024,640]{1,0:T(8,128)(2,1)S(1)} %copy-done, f32[512]{0:T(512)S(1)} %broadcast_multiply_fusion.1), kind=kOutput, calls=%fused_computation.4 | convolution fusion | flops 1326776320 | bytes 5976064 | tf_op jit(solution)/shard_map/dot_general | solution.py:23
  12.8 0.0 all-reduce.3.cloned.1.call-update
  12.8 0.0 copy-start.2
  12.8 0.0 copy-done.3
  12.9 0.1 dynamic_slice.3
  12.9 96.9 %all-reduce.3.cloned.1.call-done = f32[512,640]{1,0:T(8,128)} async-done(((f32[512,640]{1,0:T(8,128)}), f32[512,640]{1,0:T(8,128)}) %all-reduce.3.cloned.1.call-update) | async-done | bytes 1310736 | tf_op jit(solution)/shard_map/psum | solution.py:33
  109.8 0.0 copy-start.1
  109.8 1.9 %mul.96 = f32[512,640]{1,0:T(8,128)S(1)} multiply(f32[512,640]{1,0:T(8,128)} %all-reduce.3.cloned.1.call-done, f32[512,640]{1,0:T(8,128)} %all-reduce.3.cloned.1.call-done) | non-fusion elementwise | flops 327680 | bytes 3932160 | tf_op jit(solution)/shard_map/mul | solution.py:36
  111.7 0.0 copy-done.2
  111.8 0.1 copy-done.1
  111.9 1.0 fusion
  112.9 0.2 fusion.5
  113.1 8.1 %all-reduce = (f32[2,11]{0,1:T(8,128)S(1)}, f32[2,11]{0,1:T(8,128)S(1)}) all-reduce(f32[2,11]{0,1:T(8,128)S(1)} %get-tuple-element.6, f32[2,11]{0,1:T(8,128)S(1)} %get-tuple-element.5), channel_id=1, replica_groups=mesh['boot'=2,'samp'=16] {'boot'}, use_global_device_ids=true, to_apply=%region_5.6 | all-reduce | flops 44 | bytes 352 | tf_op jit(solution)/shard_map/psum | solution.py:48
  121.2 0.7 fusion.4
  (5 shorter events, 0.1 us)
Async XLA Ops:
  6.5 1.7 %copy-start = (bf16[2024,640]{1,0:T(8,128)(2,1)S(1)}, bf16[2024,640]{1,0:T(8,128)(2,1)}, u32[]{:S(2)}) copy-start(bf16[2024,640]{1,0:T(8,128)(2,1)} %param.6) | copy-start | bytes 7772164
  6.5 103.3 %all-reduce.3.cloned.1.call-start = ((), (), s32[]{:S(2)}) async-start(), calls=%async_computation | async-start | bytes 2621440 | tf_op jit(solution)/shard_map/psum | solution.py:33
  8.3 4.6 %copy-start.3 = (s32[32]{0:T(128)S(1)}, s32[32]{0:T(128)}, u32[]{:S(2)}) copy-start(s32[32]{0:T(128)} %param.9) | copy-start | bytes 388
  12.8 98.9 %copy-start.2 = (s32[512]{0:T(512)S(1)}, s32[512]{0:T(512)}, u32[]{:S(2)}) copy-start(s32[512]{0:T(512)} %param.8) | copy-start | bytes 6148
  109.8 2.1 %copy-start.1 = (f32[512,640]{1,0:T(8,128)S(1)}, f32[512,640]{1,0:T(8,128)}, u32[]{:S(2)}) copy-start(f32[512,640]{1,0:T(8,128)} %all-reduce.3.cloned.1.call-done) | copy-start | bytes 3932164
Sparse Core Ops, SparseCore 0:
  12.9 96.7 all-reduce.2
where the time goes:
time: 129 us
  waiting for transfers between devices  96.9 us (75%)
  between operations  13.4 us (10%)
  blocking collectives  8.14 us (6%)
  matrix products  5.49 us (4%)
  other arithmetic  3.86 us (3%)
    psum x1, waiting for transfers between devices, shards(): scores = lax.psum(partial_value, 'samp')  96.9 us
    psum x1, blocking collectives, shards(): lax.psum((jnp.sum(mixtures, axis=2), jnp.sum(mixtures * mixtures, axis=2)...  8.14 us
    dot_general x1, matrix products, sample_product(): lax.dot_general(dose_part, residuals, (((0,), (0,)), ((), ())), preferred...  4.52 us
  transfers between devices with their start and end apart: 1, of which 1 were waited for; matrix products, arithmetic and copies ran while one was open for 0% of the time, Pallas kernels for 0%

commit v1 on v0

--- a/solution.py
+++ b/solution.py
@@ -30,7 +30,12 @@
     scaling = variant_weights(maf_bin) / math.sqrt(sample_total)
     my_index = lax.axis_index("samp")
     partial_value = sample_product(dosage, residuals) * scaling[:, None]
-    scores = lax.psum(partial_value, "samp")
+
+    def figure_touch(mine, axis_key):
+        prior = jnp.sum(lax.all_gather(mine, axis_name=axis_key), axis=0)
+        return prior
+
+    scores = figure_touch(partial_value, "samp")
     owned_genes = lax.dynamic_slice_in_dim(gene_order, my_index * GENE_DEV, GENE_DEV)
     member = (owned_genes[:, None] == gene_map[None, :]).astype(jnp.float32)
     stacked = jnp.concatenate([scores, scores * scores], axis=1)

time: 129 us -> 153 us (1.19)
  waiting for transfers between devices: 96.9 us -> 112 us
  other arithmetic: 3.86 us -> 12.8 us
    all_gather x0 -> x1, waiting for transfers between devices: none -> 112 us  [figure_touch(): prior = jnp.sum(lax.all_gather(mine, axis_name=axis_key), axis=0)]
    psum x1 -> x0, waiting for transfers between devices: 96.9 us -> none  [shards(): scores = lax.psum(partial_value, 'samp')]
    reduce_sum x0 -> x1, other arithmetic: none -> 8.91 us  [figure_touch(): prior = jnp.sum(lax.all_gather(mine, axis_name=axis_key), axis=0)]
where the time goes in v1:
time: 153 us; the launch traced here: 152 us
  waiting for transfers between devices  112 us (73%)
  between operations  13.4 us (9%)
  other arithmetic  12.8 us (8%)
  blocking collectives  8.06 us (5%)
  matrix products  5.46 us (4%)
    all_gather x1, waiting for transfers between devices, figure_touch(): prior = jnp.sum(lax.all_gather(mine, axis_name=axis_key), axis=0)  112 us
    reduce_sum x1, other arithmetic, figure_touch(): prior = jnp.sum(lax.all_gather(mine, axis_name=axis_key), axis=0)  8.91 us
    psum x1, blocking collectives, shards(): lax.psum((jnp.sum(mixtures, axis=2), jnp.sum(mixtures * mixtures, axis=2)...  8.06 us
    dot_general x1, matrix products, sample_product(): lax.dot_general(dose_part, residuals, (((0,), (0,)), ((), ())), preferred...  4.5 us
  transfers between devices with their start and end apart: 1, of which 1 were waited for; matrix products, arithmetic and copies ran while one was open for 0% of the time, Pallas kernels for 0%

profile of v1, /device:TPU:0, one launch (start us, length us, event | category | flops | bytes accessed | tf_op | source)
XLA Modules:
  0.0 152.3 jit_solution(2033274449311123063)
XLA Ops:
  6.5 0.0 copy-start
  6.5 0.0 all-gather.3.cloned.1.call-start
  6.6 0.9 select_reduce_fusion
  7.5 0.8 copy-done
  8.3 0.0 copy-start.3
  8.3 4.5 %convolution_multiply_fusion = f32[512,640]{1,0:T(8,128)} fusion(bf16[2024,512]{1,0:T(8,128)(2,1)} %param.5, bf16[2024,640]{1,0:T(8,128)(2,1)S(1)} %copy-done, f32[512]{0:T(512)S(1)} %broadcast_multiply_fusion.1), kind=kOutput, calls=%fused_computation.4 | convolution fusion | flops 1326776320 | bytes 5976064 | tf_op jit(solution)/shard_map/dot_general | solution.py:23
  12.8 0.0 all-gather.3.cloned.1.call-update
  12.8 0.0 copy-done.3
  12.8 0.1 dynamic_slice.3
  12.9 111.5 %all-gather.3.cloned.1.call-done = f32[8192,640]{1,0:T(8,128)} async-done(((f32[512,640]{1,0:T(8,128)}), f32[8192,640]{1,0:T(8,128)}) %all-gather.3.cloned.1.call-update) | async-done | bytes 20971536 | tf_op jit(solution)/shard_map/all_gather | solution.py:35
  124.5 8.9 %reduce_sum.37 = f32[512,640]{1,0:T(8,128)} reduce(f32[16,512,640]{2,1,0:T(8,128)} %bitcast.3, f32[]{:T(128)} %constant.10.clone.1), dimensions={0}, to_apply=%region_1.2 | reduce | flops 4915200 | bytes 22282244 | tf_op jit(solution)/shard_map/reduce_sum | solution.py:35
  133.4 0.0 copy-start.1
  133.4 0.0 copy-start.2
  133.4 1.9 %mul.96 = f32[512,640]{1,0:T(8,128)S(1)} multiply(f32[512,640]{1,0:T(8,128)} %reduce_sum.37, f32[512,640]{1,0:T(8,128)} %reduce_sum.37) | non-fusion elementwise | flops 327680 | bytes 3932160 | tf_op jit(solution)/shard_map/mul | solution.py:41
  135.3 0.1 copy-done.1
  135.5 0.0 copy-done.2
  135.5 1.0 fusion
  136.4 0.2 fusion.5
  136.7 8.1 %all-reduce = (f32[2,11]{0,1:T(8,128)S(1)}, f32[2,11]{0,1:T(8,128)S(1)}) all-reduce(f32[2,11]{0,1:T(8,128)S(1)} %get-tuple-element.6, f32[2,11]{0,1:T(8,128)S(1)} %get-tuple-element.5), channel_id=1, replica_groups=mesh['boot'=2,'samp'=16] {'boot'}, use_global_device_ids=true, to_apply=%region_5.6 | all-reduce | flops 44 | bytes 352 | tf_op jit(solution)/shard_map/psum | solution.py:53
  144.7 0.7 fusion.4
  (5 shorter events, 0.1 us)
Async XLA Ops:
  6.5 1.7 %copy-start = (bf16[2024,640]{1,0:T(8,128)(2,1)S(1)}, bf16[2024,640]{1,0:T(8,128)(2,1)}, u32[]{:S(2)}) copy-start(bf16[2024,640]{1,0:T(8,128)(2,1)} %param.6) | copy-start | bytes 7772164
  6.5 117.9 %all-gather.3.cloned.1.call-start = ((), (), s32[]{:S(2)}) async-start(), calls=%async_computation | async-start | bytes 22282240 | tf_op jit(solution)/shard_map/all_gather | solution.py:35
  8.3 4.5 %copy-start.3 = (s32[32]{0:T(128)S(1)}, s32[32]{0:T(128)}, u32[]{:S(2)}) copy-start(s32[32]{0:T(128)} %param.9) | copy-start | bytes 388
  133.4 2.1 %copy-start.1 = (f32[512,640]{1,0:T(8,128)S(1)}, f32[512,640]{1,0:T(8,128)}, u32[]{:S(2)}) copy-start(f32[512,640]{1,0:T(8,128)} %reduce_sum.37) | copy-start | bytes 3932164
  133.4 2.1 %copy-start.2 = (s32[512]{0:T(512)S(1)}, s32[512]{0:T(512)}, u32[]{:S(2)}) copy-start(s32[512]{0:T(512)} %param.8) | copy-start | bytes 6148
Sparse Core Ops, SparseCore 0:
  12.9 111.4 all-gather.2
